TPU v7x, 32 devices: a whole 2x2x4 slice. The times are simulated.
32 devices in a mesh: grp: 8 (over y, x, core), blk: 4 (over z).
Axes of the slice: x: 2, y: 2, z: 4, core: 2. Of those that a mesh axis runs over, the one named last changes fastest.
Arguments:
- image_tokens: bfloat16 [3, 7168, 2432], P(None, ('grp', 'blk')), may hold values from -128 to 128, as said below
- text_tokens: bfloat16 [3, 512, 2432], P(None, ('grp', 'blk')), may hold values from -128 to 128, as said below
- lengths: int32 [8], P('grp'), may hold values from 224 to 896
- image_weight: bfloat16 [2432, 2432], P('grp'), may hold values from -0.125 to 0.125
- text_weight: bfloat16 [2432, 2432], P('grp'), may hold values from -0.125 to 0.125
- gate_values: float32 [8, 2, 2432], P('grp'), may hold values from 0.5 to 2
Outputs:
- image_update: bfloat16 [7168, 2432], P(('grp', 'blk'))
- text_update: bfloat16 [512, 2432], P(('grp', 'blk'))
Inputs may be any that keep to these rules, and one draw needn't show every extreme that they name: `image_tokens`: Real-valued queries, keys and values. `text_tokens`: Real-valued queries, keys and values. Request g has lengths[g] image tokens; its slots from that index up to 896 are padding, never valid keys.
All inputs are finite; a program needn't handle non-finite values.
Results may differ from a plain program's by a relative error of at most 0.0085.
Values may be sent and summed in bfloat16 or wider, within the bound.
A program may use at most 256 MiB of HBM per device.

v0:
```python
import jax
import jax.numpy as jnp
from jax import lax
from jax.sharding import PartitionSpec as P

HEADS = 38


NEG_FILL = -1e30


def key_mask(row_count, image_rows, text_rows, length):
    row_ids = jnp.arange(row_count, dtype=jnp.int32)
    shard_span = image_rows + text_rows
    shard_idx = row_ids // shard_span
    within = row_ids % shard_span
    return (within >= image_rows) | (shard_idx * image_rows + within < length)


def empty_state(query_count, head_count, head_size):
    return (
        jnp.full((query_count, head_count), NEG_FILL, jnp.float32),
        jnp.zeros((query_count, head_count), jnp.float32),
        jnp.zeros((query_count, head_count, head_size), jnp.float32),
    )


def softmax_step(running, queries, key_rows, value_rows, usable):
    maxima, totals, weighted = running
    query_count, head_count, head_size = weighted.shape
    scores = jnp.einsum(
        "qhd,khd->qhk", queries, key_rows, preferred_element_type=jnp.float32
    ) * head_size ** (-0.5)
    scores = jnp.where(usable[None, None, :], scores, NEG_FILL)
    new_max = jnp.maximum(maxima, jnp.max(scores, axis=-1))
    probs = jnp.where(usable[None, None, :], jnp.exp(scores - new_max[:, :, None]), 0.0)
    new_totals = jnp.sum(probs, axis=-1)
    update = jnp.einsum(
        "qhk,khd->qhd", probs.astype(jnp.bfloat16), value_rows, preferred_element_type=jnp.float32
    )
    return (new_max, new_totals, update)


def normalize(running):
    maxima, totals, weighted = running
    query_count = weighted.shape[0]
    return (weighted / totals[:, :, None]).reshape(query_count, -1).astype(jnp.bfloat16)


def contract_with(left_image, left_text, pieces):
    return (
        jnp.dot(left_image, pieces[0], preferred_element_type=jnp.float32),
        jnp.dot(left_text, pieces[1], preferred_element_type=jnp.float32),
    )


def per_device(image_tokens, text_tokens, lengths, image_weight, text_weight, gate_values):
    image_rows = image_tokens.shape[1]
    text_rows = text_tokens.shape[1]
    model_width = image_tokens.shape[2]
    head_size = model_width // HEADS
    length = lengths[0]
    members = lax.axis_size("blk")
    per_member = -(-HEADS // members)
    padded_heads = per_member * members
    stacked = jnp.concatenate([image_tokens, text_tokens], axis=1)
    stacked = jnp.pad(stacked, ((0, 0), (0, 0), (0, padded_heads * head_size - model_width)))
    stacked = stacked.reshape(3, image_rows + text_rows, members, per_member, head_size)
    all_rows = (image_rows + text_rows) * members
    usable = key_mask(all_rows, image_rows, text_rows, length)

    def one_head(triple):
        state = softmax_step(
            empty_state(all_rows, 1, head_size),
            triple[0][:, None, :],
            triple[1][:, None, :],
            triple[2][:, None, :],
            usable,
        )
        return normalize(state)

    moved = jnp.moveaxis(
        lax.all_to_all(stacked, "blk", split_axis=2, concat_axis=1, tiled=True)[:, :, 0], 2, 0
    )
    results = lax.map(one_head, moved)
    head_out = jnp.moveaxis(results, 0, 1)[:, None]
    back = lax.all_to_all(head_out, "blk", split_axis=0, concat_axis=1, tiled=True)
    attended = back.reshape(image_rows + text_rows, padded_heads * head_size)[:, :model_width]
    image_attended = attended[:image_rows]
    text_attended = attended[image_rows:]
    image_gate = gate_values[0, 0]
    text_gate = gate_values[0, 1]
    image_sum, text_sum = contract_with(
        image_attended,
        text_attended,
        (
            lax.all_gather(image_weight, "grp", axis=0, tiled=True),
            lax.all_gather(text_weight, "grp", axis=0, tiled=True),
        ),
    )
    image_update = (image_sum * image_gate).astype(jnp.bfloat16)
    text_update = (text_sum * text_gate).astype(jnp.bfloat16)
    return (image_update, text_update)


def solution(mesh):
    in_specs = (
        P(None, ("grp", "blk"), None),
        P(None, ("grp", "blk"), None),
        P("grp"),
        P("grp", None),
        P("grp", None),
        P("grp", None, None),
    )
    out_specs = (P(("grp", "blk"), None), P(("grp", "blk"), None))
    return jax.shard_map(
        per_device, mesh=mesh, in_specs=in_specs, out_specs=out_specs, check_vma=False
    )
```

profile of v0, /device:TPU:0, one launch (start us, length us, event | category | flops | bytes accessed | tf_op | source)
XLA Modules:
  0.0 290.5 jit_solution(11370722174082935025)
XLA Ops:
  7.9 5.8 %copy.17 = bf16[3,224,2432]{1,2,0:T(8,128)(2,1)} copy(bf16[3,224,2432]{2,1,0:T(8,128)(2,1)} %param.8) | data formatting | bytes 6537216 | tf_op args[0]
  15.0 4.2 %fusion.42 = bf16[3,240,2560]{1,2,0:T(8,128)(2,1)S(1)} fusion(bf16[3,16,2432]{1,2,0:T(8,128)(2,1)S(1)} %copy.18, bf16[3,224,2432]{1,2,0:T(8,128)(2,1)} %copy.17), kind=kLoop, calls=%fused_computation.43 | loop fusion | flops 12902400 | bytes 7188480 | tf_op jit(solution)/shard_map/concatenate | solution.py:66
  21.4 6.3 %all-to-all-start = ((bf16[3,240,4,10,64]{1,4,3,0,2:T(8,128)(2,1)}), bf16[3,240,4,10,64]{1,4,3,0,2:T(8,128)(2,1)}, u32[]{:S(2)}, u32[]{:S(2)}) async-start(bf16[3,240,4,10,64]{1,4,3,0,2:T(8,128)(2,1)} %copy.19), calls=%async_computation | async-start | bytes 7864320 | tf_op jit(solution)/shard_map/all_to_all | solution.py:83
  28.5 87.1 %all-to-all-done = bf16[3,240,4,10,64]{1,4,3,0,2:T(8,128)(2,1)} async-done(((bf16[3,240,4,10,64]{1,4,3,0,2:T(8,128)(2,1)}), bf16[3,240,4,10,64]{1,4,3,0,2:T(8,128)(2,1)}, u32[]{:S(2)}, u32[]{:S(2)}) %all-to-all-start) | async-done | bytes 3686432 | tf_op jit(solution)/shard_map/all_to_all | solution.py:83
  115.6 9.0 %copy.20 = bf16[3,4,240,1,10,64]{2,1,5,4,0,3:T(4,128)(2,1)} copy(bf16[3,4,240,1,10,64]{2,5,4,0,1,3:T(8,128)(2,1)} %bitcast.2) | data formatting | bytes 7372800 | tf_op jit(solution)/shard_map/all_to_all | solution.py:83
  124.6 8.6 %squeeze.6 = bf16[3,960,10,64]{1,3,2,0:T(8,128)(2,1)} reshape(bf16[3,4,240,1,10,64]{2,1,5,4,0,3:T(4,128)(2,1)} %copy.20) | data formatting | bytes 7372800 | tf_op jit(solution)/shard_map/squeeze | solution.py:83
  133.2 86.4 %while.11 = (s32[]{:T(128)}, bf16[10,960,64]{1,2,0:T(8,128)(2,1)S(1)}, bf16[10,3,960,64]{2,3,0,1:T(8,128)(2,1)}, s32[]{:T(128)}, s32[]{:T(128)}, /*index=5*/s32[]{:T(128)}, s32[]{}, s32[]{}) while((s32[]{:T(128)}, bf16[10,960,64]{1,2,0:T(8,128)(2,1)S(1)}, bf16[10,3,960,64]{2,3,0,1:T(8,128)(2,1)}, s32[]{:T(128)}, s32[]{:T(128)}, ...), condition=%wide.region_3.4_spmd.clone, body=%wide.region_0.3_spmd.clone.sunk | while | flops 248048640 | bytes 26608340 | solution.py:85
  138.6 3.3 %fusion.58 = bf16[10,960,64]{1,2,0:T(8,128)(2,1)S(1)} fusion(bf16[10,960,64]{1,2,0:T(8,128)(2,1)S(1)} %get-tuple-element.94, s32[]{:T(128)} %get-tuple-element.93, f32[960,960]{1,0:T(8,128)} %copy-done, f32[960]{0:T(1024)S(1)} %broadcast_maximum_fusion.2, pred[960]{0:T(1024)(128)(4,1)S(1)} %fusion.55, ...), kind=kOutput, calls=%fused_computation.13.clone.1 | convolution fusion | flops 122695680 | bytes 4204548 | tf_op jit(solution)/shard_map/while/body/eval_jaxpr/qhk,khd->qhd/dot_general | solution.py:38
  147.2 3.3 %fusion.58 = bf16[10,960,64]{1,2,0:T(8,128)(2,1)S(1)} fusion(bf16[10,960,64]{1,2,0:T(8,128)(2,1)S(1)} %get-tuple-element.94, s32[]{:T(128)} %get-tuple-element.93, f32[960,960]{1,0:T(8,128)} %copy-done, f32[960]{0:T(1024)S(1)} %broadcast_maximum_fusion.2, pred[960]{0:T(1024)(128)(4,1)S(1)} %fusion.55, ...), kind=kOutput, calls=%fused_computation.13.clone.1 | convolution fusion | flops 122695680 | bytes 4204548 | tf_op jit(solution)/shard_map/while/body/eval_jaxpr/qhk,khd->qhd/dot_general | solution.py:38
  155.9 3.3 %fusion.58 = bf16[10,960,64]{1,2,0:T(8,128)(2,1)S(1)} fusion(bf16[10,960,64]{1,2,0:T(8,128)(2,1)S(1)} %get-tuple-element.94, s32[]{:T(128)} %get-tuple-element.93, f32[960,960]{1,0:T(8,128)} %copy-done, f32[960]{0:T(1024)S(1)} %broadcast_maximum_fusion.2, pred[960]{0:T(1024)(128)(4,1)S(1)} %fusion.55, ...), kind=kOutput, calls=%fused_computation.13.clone.1 | convolution fusion | flops 122695680 | bytes 4204548 | tf_op jit(solution)/shard_map/while/body/eval_jaxpr/qhk,khd->qhd/dot_general | solution.py:38
  164.5 3.3 %fusion.58 = bf16[10,960,64]{1,2,0:T(8,128)(2,1)S(1)} fusion(bf16[10,960,64]{1,2,0:T(8,128)(2,1)S(1)} %get-tuple-element.94, s32[]{:T(128)} %get-tuple-element.93, f32[960,960]{1,0:T(8,128)} %copy-done, f32[960]{0:T(1024)S(1)} %broadcast_maximum_fusion.2, pred[960]{0:T(1024)(128)(4,1)S(1)} %fusion.55, ...), kind=kOutput, calls=%fused_computation.13.clone.1 | convolution fusion | flops 122695680 | bytes 4204548 | tf_op jit(solution)/shard_map/while/body/eval_jaxpr/qhk,khd->qhd/dot_general | solution.py:38
  181.8 3.3 %fusion.58 = bf16[10,960,64]{1,2,0:T(8,128)(2,1)S(1)} fusion(bf16[10,960,64]{1,2,0:T(8,128)(2,1)S(1)} %get-tuple-element.94, s32[]{:T(128)} %get-tuple-element.93, f32[960,960]{1,0:T(8,128)} %copy-done, f32[960]{0:T(1024)S(1)} %broadcast_maximum_fusion.2, pred[960]{0:T(1024)(128)(4,1)S(1)} %fusion.55, ...), kind=kOutput, calls=%fused_computation.13.clone.1 | convolution fusion | flops 122695680 | bytes 4204548 | tf_op jit(solution)/shard_map/while/body/eval_jaxpr/qhk,khd->qhd/dot_general | solution.py:38
  190.4 3.3 %fusion.58 = bf16[10,960,64]{1,2,0:T(8,128)(2,1)S(1)} fusion(bf16[10,960,64]{1,2,0:T(8,128)(2,1)S(1)} %get-tuple-element.94, s32[]{:T(128)} %get-tuple-element.93, f32[960,960]{1,0:T(8,128)} %copy-done, f32[960]{0:T(1024)S(1)} %broadcast_maximum_fusion.2, pred[960]{0:T(1024)(128)(4,1)S(1)} %fusion.55, ...), kind=kOutput, calls=%fused_computation.13.clone.1 | convolution fusion | flops 122695680 | bytes 4204548 | tf_op jit(solution)/shard_map/while/body/eval_jaxpr/qhk,khd->qhd/dot_general | solution.py:38
  199.0 3.3 %fusion.58 = bf16[10,960,64]{1,2,0:T(8,128)(2,1)S(1)} fusion(bf16[10,960,64]{1,2,0:T(8,128)(2,1)S(1)} %get-tuple-element.94, s32[]{:T(128)} %get-tuple-element.93, f32[960,960]{1,0:T(8,128)} %copy-done, f32[960]{0:T(1024)S(1)} %broadcast_maximum_fusion.2, pred[960]{0:T(1024)(128)(4,1)S(1)} %fusion.55, ...), kind=kOutput, calls=%fused_computation.13.clone.1 | convolution fusion | flops 122695680 | bytes 4204548 | tf_op jit(solution)/shard_map/while/body/eval_jaxpr/qhk,khd->qhd/dot_general | solution.py:38
  207.7 3.3 %fusion.58 = bf16[10,960,64]{1,2,0:T(8,128)(2,1)S(1)} fusion(bf16[10,960,64]{1,2,0:T(8,128)(2,1)S(1)} %get-tuple-element.94, s32[]{:T(128)} %get-tuple-element.93, f32[960,960]{1,0:T(8,128)} %copy-done, f32[960]{0:T(1024)S(1)} %broadcast_maximum_fusion.2, pred[960]{0:T(1024)(128)(4,1)S(1)} %fusion.55, ...), kind=kOutput, calls=%fused_computation.13.clone.1 | convolution fusion | flops 122695680 | bytes 4204548 | tf_op jit(solution)/shard_map/while/body/eval_jaxpr/qhk,khd->qhd/dot_general | solution.py:38
  216.3 3.3 %fusion.58 = bf16[10,960,64]{1,2,0:T(8,128)(2,1)S(1)} fusion(bf16[10,960,64]{1,2,0:T(8,128)(2,1)S(1)} %get-tuple-element.94, s32[]{:T(128)} %get-tuple-element.93, f32[960,960]{1,0:T(8,128)} %copy-done, f32[960]{0:T(1024)S(1)} %broadcast_maximum_fusion.2, pred[960]{0:T(1024)(128)(4,1)S(1)} %fusion.55, ...), kind=kOutput, calls=%fused_computation.13.clone.1 | convolution fusion | flops 122695680 | bytes 4204548 | tf_op jit(solution)/shard_map/while/body/eval_jaxpr/qhk,khd->qhd/dot_general | solution.py:38
  219.6 4.8 %copy.22 = bf16[10,960,64]{2,0,1:T(8,128)(2,1)} copy(bf16[10,960,64]{1,2,0:T(8,128)(2,1)S(1)} %get-tuple-element.24) | data formatting | bytes 2457600 | tf_op jit(solution)/shard_map/while | solution.py:85
  224.4 4.9 %reshape.76 = bf16[4,2,76800]{2,1,0:T(2,128)(2,1)} reshape(bf16[960,1,10,64]{3,2,1,0:T(8,128)(2,1)} %bitcast.106) | data formatting | bytes 2457600
  229.3 3.7 %all-to-all-start.1 = ((bf16[4,2,76800]{2,1,0:T(2,128)(2,1)}), bf16[4,2,76800]{2,1,0:T(2,128)(2,1)S(1)}, u32[]{:S(2)}, u32[]{:S(2)}) async-start(bf16[4,2,76800]{2,1,0:T(2,128)(2,1)} %reshape.76), calls=%async_computation.1 | async-start | bytes 2457600 | tf_op jit(solution)/shard_map/all_to_all | solution.py:87
  233.1 27.7 %all-to-all-done.1 = bf16[4,2,76800]{2,1,0:T(2,128)(2,1)S(1)} async-done(((bf16[4,2,76800]{2,1,0:T(2,128)(2,1)}), bf16[4,2,76800]{2,1,0:T(2,128)(2,1)S(1)}, u32[]{:S(2)}, u32[]{:S(2)}) %all-to-all-start.1) | async-done | bytes 1228832 | tf_op jit(solution)/shard_map/all_to_all | solution.py:87
  260.8 3.5 %reshape.77 = bf16[960,1,10,64]{3,2,1,0:T(8,128)(2,1)} reshape(bf16[4,2,76800]{2,1,0:T(2,128)(2,1)S(1)} %all-to-all-done.1) | data formatting | bytes 2457600
  264.3 4.0 %copy.23 = bf16[4,240,1,10,64]{1,4,3,0,2:T(8,128)(2,1)S(1)} copy(bf16[4,240,1,10,64]{4,3,1,0,2:T(8,128)(2,1)} %bitcast.107) | data formatting | bytes 2457600 | tf_op jit(solution)/shard_map/all_to_all | solution.py:87
  268.4 8.5 %fusion.43 = bf16[224,2432]{1,0:T(8,128)(2,1)} fusion(bf16[2432,2432]{1,0:T(8,128)(2,1)} %all-gather.3.cloned.1.call-done, bf16[240,2560]{0,1:T(8,128)(2,1)S(1)} %bitcast.108, f32[2432]{0:T(1024)S(1)} %get-tuple-element.45), kind=kOutput, calls=%fused_computation.44 | convolution fusion | flops 2650841088 | bytes 14176256 | tf_op jit(solution)/shard_map/dot_general | solution.py:52
  276.9 6.8 %fusion.44 = bf16[16,2432]{1,0:T(8,128)(2,1)} fusion(bf16[2432,2432]{1,0:T(8,128)(2,1)} %all-gather.5.cloned.1.call-done, bf16[240,2560]{0,1:T(8,128)(2,1)S(1)} %bitcast.109, f32[2432]{0:T(1024)S(1)} %get-tuple-element.44), kind=kOutput, calls=%fused_computation.46 | convolution fusion | flops 189345792 | bytes 12541952 | tf_op jit(solution)/shard_map/dot_general | solution.py:53
  (75 shorter events, 61.5 us)
Async XLA Ops:
  7.2 6.6 %copy-start.1 = (bf16[3,16,2432]{2,1,0:T(8,128)(2,1)S(1)}, bf16[3,16,2432]{2,1,0:T(8,128)(2,1)}, u32[]{:S(2)}) copy-start(bf16[3,16,2432]{2,1,0:T(8,128)(2,1)} %param.9) | copy-start | bytes 700420
  7.2 261.2 %all-gather.3.cloned.1.call-start = ((), (), s32[]{:S(2)}) async-start(), calls=%async_computation.2 | async-start | bytes 13307904 | tf_op jit(solution)/shard_map/all_gather | solution.py:97
  21.4 94.2 %all-to-all-start = ((bf16[3,240,4,10,64]{1,4,3,0,2:T(8,128)(2,1)}), bf16[3,240,4,10,64]{1,4,3,0,2:T(8,128)(2,1)}, u32[]{:S(2)}, u32[]{:S(2)}) async-start(bf16[3,240,4,10,64]{1,4,3,0,2:T(8,128)(2,1)} %copy.19), calls=%async_computation | async-start | bytes 7864320 | tf_op jit(solution)/shard_map/all_to_all | solution.py:83
  27.8 249.1 %all-gather.5.cloned.1.call-start = ((), (), s32[]{:S(2)}) async-start(), calls=%async_computation.3 | async-start | bytes 13307904 | tf_op jit(solution)/shard_map/all_gather | solution.py:98
  135.6 2.0 copy-start
  144.3 2.0 copy-start
  152.9 2.0 copy-start
  161.5 2.0 copy-start
  170.2 2.0 copy-start
  178.8 2.0 copy-start
  187.4 2.0 copy-start
  196.1 2.0 copy-start
  204.7 2.0 copy-start
  213.3 2.0 copy-start
  224.4 8.7 %copy-start.2 = (f32[1,2,2432]{2,1,0:T(2,128)S(1)}, f32[1,2,2432]{2,1,0:T(2,128)}, u32[]{:S(2)}) copy-start(f32[1,2,2432]{2,1,0:T(2,128)} %param.13) | copy-start | bytes 58372
  229.3 31.5 %all-to-all-start.1 = ((bf16[4,2,76800]{2,1,0:T(2,128)(2,1)}), bf16[4,2,76800]{2,1,0:T(2,128)(2,1)S(1)}, u32[]{:S(2)}, u32[]{:S(2)}) async-start(bf16[4,2,76800]{2,1,0:T(2,128)(2,1)} %reshape.76), calls=%async_computation.1 | async-start | bytes 2457600 | tf_op jit(solution)/shard_map/all_to_all | solution.py:87
Sparse Core Ops, SparseCore 0:
  9.9 71.5 all-gather.2
  83.3 68.7 all-gather.4
where the time goes:
time: 292 us; the launch traced here: 291 us
  waiting for transfers between devices  116 us (40%)
  matrix products  65 us (22%)
  local copies, waits for them, and re-layouts  63.8 us (22%)
  other arithmetic  20.8 us (7%)
  between operations  14.1 us (5%)
  starting transfers between devices  10.1 us (3%)
    all_to_all x1, waiting for transfers between devices, per_device(): lax.all_to_all(stacked, 'blk', split_axis=2, concat_axis=1, tiled=True)  87.1 us
    dot_general x10, matrix products, softmax_step(): jnp.einsum('qhk,khd->qhd', probs.astype(jnp.bfloat16), value_rows, prefer...  32.8 us
    all_to_all x1, waiting for transfers between devices, per_device(): lax.all_to_all(head_out, 'blk', split_axis=0, concat_axis=1, tiled=True)  27.7 us
    while x20, local copies, waits for them, and re-layouts  19.5 us
    dot_general x10, matrix products, softmax_step(): jnp.einsum('qhd,khd->qhk', queries, key_rows, preferred_element_type=jnp....  16.9 us
    unnamed x8, local copies, waits for them, and re-layouts  15.6 us
    reduce_sum x10, other arithmetic, softmax_step(): new_totals = jnp.sum(probs, axis=-1)  10 us
    all_to_all x1, local copies, waits for them, and re-layouts, per_device(): lax.all_to_all(stacked, 'blk', split_axis=2, concat_axis=1, tiled=True)  8.96 us
  transfers between devices with their start and end apart: 4, of which 2 were waited for; matrix products, arithmetic and copies ran while one was open for 42% of the time, Pallas kernels for 0%

commit v1 on v0

v1 whole, which is shorter than its diff:
```python
import functools

import jax
import jax.numpy as jnp
from jax import lax
from jax.experimental import pallas as pl
from jax.experimental.pallas import tpu as pltpu
from jax.sharding import PartitionSpec as P

HEADS = 38
NEG_FILL = -1e30
LANES = 128
MESH = pl.DeviceIdType.MESH


def key_mask(row_count, image_rows, text_rows, length):
    row_ids = jnp.arange(row_count, dtype=jnp.int32)
    shard_span = image_rows + text_rows
    shard_idx = row_ids // shard_span
    within = row_ids % shard_span
    return (within >= image_rows) | (shard_idx * image_rows + within < length)


def exchange_kernel(
    n, head_size,
    img, txt, bias, out_img, out_txt,
    qkv, done_img, done_txt,
    in_send, in_recv, in_local, out_send, out_recv, out_local,
):
    me = lax.axis_index("blk")
    image_rows, text_rows = img.shape[1], txt.shape[1]
    span = image_rows + text_rows
    pairs = img.shape[2] // LANES
    base, extra = divmod(pairs, n)
    most = qkv.shape[0]

    def count(b):
        return base + jnp.where(b < extra, 1, 0)

    def columns(b, p):
        return pl.ds(pl.multiple_of((b * base + jnp.minimum(b, extra) + p) * LANES, LANES), LANES)

    def image_slot(p, b):
        return qkv.at[p, :, pl.ds(pl.multiple_of(b * span, 16), image_rows), :]

    def text_slot(p, b):
        return qkv.at[p, :, pl.ds(pl.multiple_of(b * span + image_rows, 16), text_rows), :]

    barrier = pltpu.get_barrier_semaphore()
    for d in range(1, n):
        pl.semaphore_signal(barrier, inc=1, device_id={"blk": lax.rem(me + d, n)}, device_id_type=MESH)
    pl.semaphore_wait(barrier, n - 1)

    def in_copies(p, dest, owner, d):
        cols = columns(dest, p)
        return [
            pltpu.make_async_remote_copy(
                src_ref=src.at[:, :, cols], dst_ref=slot(p, owner),
                send_sem=in_send.at[p, d, i], recv_sem=in_recv.at[p, owner, i],
                device_id={"blk": dest}, device_id_type=MESH)
            for i, (src, slot) in enumerate(((img, image_slot), (txt, text_slot)))
        ]

    def own_copies(p):
        cols = columns(me, p)
        return [
            pltpu.make_async_copy(src.at[:, :, cols], slot(p, me), in_local.at[p, i])
            for i, (src, slot) in enumerate(((img, image_slot), (txt, text_slot)))
        ]

    def image_out(p, dest, owner, d):
        return pltpu.make_async_remote_copy(
            src_ref=done_img.at[p, dest], dst_ref=out_img.at[:, columns(owner, p)],
            send_sem=out_send.at[p, d, 0], recv_sem=out_recv.at[p, owner, 0],
            device_id={"blk": dest}, device_id_type=MESH)

    def text_out(p, dest, owner, d):
        return pltpu.make_async_remote_copy(
            src_ref=done_txt.at[p], dst_ref=out_txt.at[:, columns(owner, p)],
            send_sem=out_send.at[p, d, 1], recv_sem=out_recv.at[p, owner, 1],
            device_id={"blk": dest}, device_id_type=MESH)

    def image_own(p):
        return pltpu.make_async_copy(done_img.at[p, me], out_img.at[:, columns(me, p)], out_local.at[p, 0])

    def text_own(p):
        return pltpu.make_async_copy(done_txt.at[p], out_txt.at[:, columns(me, p)], out_local.at[p, 1])

    for p in range(most):
        for d in range(1, n):
            dest = lax.rem(me + d, n)

            @pl.when(p < count(dest))
            def _():
                for copy in in_copies(p, dest, me, d):
                    copy.start()

        @pl.when(p < count(me))
        def _():
            for copy in own_copies(p):
                copy.start()

    first = lax.broadcasted_iota(jnp.int32, (span, LANES), 1) < head_size
    scale = head_size ** (-0.5)

    def one_pair(p, _):
        for copy in own_copies(p):
            copy.wait()
        for d in range(1, n):
            for copy in in_copies(p, me, lax.rem(me + d, n), d):
                copy.wait_recv()

        def one_block(j, _):
            dest = lax.rem(me + 1 + j, n)
            rows = pl.ds(pl.multiple_of(dest * span, 16), span)
            queries = qkv[p, 0, rows, :]
            halves = []
            for h in range(2):
                own = first if h == 0 else jnp.logical_not(first)
                q_h = jnp.where(own, queries, jnp.zeros_like(queries))
                scores = lax.dot_general(
                    q_h, qkv[p, 1], (((1,), (1,)), ((), ())), preferred_element_type=jnp.float32
                ) * scale + bias[...]
                weights = jnp.exp(scores - jnp.max(scores, axis=1, keepdims=True))
                totals = jnp.sum(weights, axis=1, keepdims=True)
                summed = jnp.dot(weights.astype(jnp.bfloat16), qkv[p, 2], preferred_element_type=jnp.float32)
                halves.append(summed / totals)
            out = jnp.where(first, halves[0], halves[1]).astype(jnp.bfloat16)
            done_img[p, dest] = out[:image_rows]
            done_txt[p, pl.ds(pl.multiple_of(dest * text_rows, 16), text_rows), :] = out[image_rows:]

            @pl.when(j < n - 1)
            def _():
                image_out(p, dest, me, j + 1).start()

            return 0

        lax.fori_loop(0, n, one_block, 0)
        image_own(p).start()
        text_own(p).start()
        for d in range(1, n):
            text_out(p, lax.rem(me + d, n), me, d).start()
        return 0

    lax.fori_loop(0, count(me), one_pair, 0)

    for p in range(most):
        for d in range(1, n):
            peer = lax.rem(me + d, n)

            @pl.when(p < count(peer))
            def _():
                for copy in in_copies(p, peer, me, d):
                    copy.wait_send()
                image_out(p, me, peer, d).wait_recv()
                text_out(p, me, peer, d).wait_recv()

            @pl.when(p < count(me))
            def _():
                image_out(p, peer, me, d).wait_send()
                text_out(p, peer, me, d).wait_send()

        @pl.when(p < count(me))
        def _():
            image_own(p).wait()
            text_own(p).wait()


def attend(image_tokens, text_tokens, bias, n, head_size):
    image_rows, text_rows, width = image_tokens.shape[1], text_tokens.shape[1], image_tokens.shape[2]
    span = image_rows + text_rows
    most = -(-(width // LANES) // n)
    dma = pltpu.SemaphoreType.DMA
    any_space = pl.BlockSpec(memory_space=pl.ANY)
    return pl.pallas_call(
        functools.partial(exchange_kernel, n, head_size),
        out_shape=(
            jax.ShapeDtypeStruct((image_rows, width), jnp.bfloat16),
            jax.ShapeDtypeStruct((n * text_rows, width), jnp.bfloat16),
        ),
        in_specs=[any_space, any_space, pl.BlockSpec(memory_space=pltpu.VMEM)],
        out_specs=(any_space, any_space),
        scratch_shapes=[
            pltpu.VMEM((most, 3, n * span, LANES), jnp.bfloat16),
            pltpu.VMEM((most, n, image_rows, LANES), jnp.bfloat16),
            pltpu.VMEM((most, n * text_rows, LANES), jnp.bfloat16),
            dma((most, n, 2)), dma((most, n, 2)), dma((most, 2)),
            dma((most, n, 2)), dma((most, n, 2)), dma((most, 2)),
        ],
        compiler_params=pltpu.CompilerParams(
            collective_id=0, has_side_effects=True, vmem_limit_bytes=48 * 1024 * 1024
        ),
        name="attend",
    )(image_tokens, text_tokens, bias)


def per_device(image_tokens, text_tokens, lengths, image_weight, text_weight, gate_values):
    image_rows = image_tokens.shape[1]
    text_rows = text_tokens.shape[1]
    width = image_tokens.shape[2]
    n = lax.axis_size("blk")
    me = lax.axis_index("blk")
    share = width // n
    usable = key_mask((image_rows + text_rows) * n, image_rows, text_rows, lengths[0])
    bias = jnp.where(usable, 0.0, NEG_FILL).astype(jnp.float32)[None, :]
    own_text = lax.dynamic_slice_in_dim(text_weight, me * share, share, axis=1)
    image_full = lax.all_gather(image_weight, "grp", axis=0, tiled=True)
    text_full = lax.all_gather(own_text, "grp", axis=0, tiled=True)
    image_attended, text_attended = attend(image_tokens, text_tokens, bias, n, width // HEADS)
    text_gate = lax.dynamic_slice_in_dim(gate_values[0, 1], me * share, share, axis=0)
    text_part = (
        jnp.dot(text_attended, text_full, preferred_element_type=jnp.float32) * text_gate
    ).astype(jnp.bfloat16)
    text_update = lax.all_to_all(text_part, "blk", split_axis=0, concat_axis=1, tiled=True)
    image_update = (
        jnp.dot(image_attended, image_full, preferred_element_type=jnp.float32) * gate_values[0, 0]
    ).astype(jnp.bfloat16)
    return (image_update, text_update)


def solution(mesh):
    in_specs = (
        P(None, ("grp", "blk"), None),
        P(None, ("grp", "blk"), None),
        P("grp"),
        P("grp", None),
        P("grp", None),
        P("grp", None, None),
    )
    out_specs = (P(("grp", "blk"), None), P(("grp", "blk"), None))
    return jax.shard_map(
        per_device, mesh=mesh, in_specs=in_specs, out_specs=out_specs, check_vma=False
    )
```

time: 292 us -> 155 us (0.53)
  waiting for transfers between devices: 116 us -> 0.73 us
  Pallas kernels: 0 us -> 115 us
  local copies, waits for them, and re-layouts: 63.8 us -> 5.08 us
  matrix products: 65 us -> 11.1 us
  other arithmetic: 20.8 us -> 0.03 us
  starting transfers between devices: 10.1 us -> 0.08 us
  blocking collectives: 0 us -> 8.16 us
    pallas_call x0 -> x1, Pallas kernels: none -> 115 us  [attend(): pl.pallas_call(functools.partial(exchange_kernel, n, head_size), out_shap...]
    all_to_all x2 -> x0, waiting for transfers between devices: 115 us -> none  [the longest x1 87.1 us: per_device(): lax.all_to_all(stacked, 'blk', split_axis=2, concat_axis=1, tiled=True)]
    dot_general x22 -> x2, matrix products: 65 us -> 11.1 us  [the longest x1 8.52 us: per_device(): jnp.dot(image_attended, image_full, preferred_element_type=jnp.float32)]
    while x21 -> x0, local copies, waits for them, and re-layouts: 24.3 us -> none
    unnamed x8, local copies, waits for them, and re-layouts: 15.6 us -> 3.24 us
    all_to_all x2, local copies, waits for them, and re-layouts: 13 us -> 0.79 us  [per_device(): lax.all_to_all(text_part, 'blk', split_axis=0, concat_axis=1, tiled=True)]
    all_to_all x2 -> x0, starting transfers between devices: 10.1 us -> none  [the longest x1 6.35 us: per_device(): lax.all_to_all(stacked, 'blk', split_axis=2, concat_axis=1, tiled=True)]
    reduce_sum x10 -> x0, other arithmetic: 10 us -> none  [softmax_step(): new_totals = jnp.sum(probs, axis=-1)]
  transfers between devices with their start and end apart: 4 -> 2, of which waited for: 2 -> 0; matrix products, arithmetic and copies ran while one was open for 42% -> 2% of each run, Pallas kernels for 0% -> 74%
where the time goes in v1:
time: 155 us
  Pallas kernels  115 us (74%)
  between operations  14.8 us (10%)
  matrix products  11.1 us (7%)
  blocking collectives  8.16 us (5%)
  local copies, waits for them, and re-layouts  5.08 us (3%)
    pallas_call x1, Pallas kernels, attend(): pl.pallas_call(functools.partial(exchange_kernel, n, head_size), out_shap...  115 us
    dot_general x1, matrix products, per_device(): jnp.dot(image_attended, image_full, preferred_element_type=jnp.float32)  8.52 us
    all_to_all x1, blocking collectives, per_device(): lax.all_to_all(text_part, 'blk', split_axis=0, concat_axis=1, tiled=True)  8.16 us
    unnamed x8, local copies, waits for them, and re-layouts  3.24 us
  transfers between devices with their start and end apart: 2, of which 0 were waited for; matrix products, arithmetic and copies ran while one was open for 2% of the time, Pallas kernels for 74%

profile of v1, /device:TPU:0, one launch (start us, length us, event | category | flops | bytes accessed | tf_op | source)
XLA Modules:
  0.0 154.8 jit_solution(9001227140155485079)
XLA Ops:
  7.2 0.0 copy-start
  7.2 0.0 copy-start.2
  7.2 0.0 all-gather.5.cloned.1.call-start
  7.2 1.3 copy-done
  8.5 0.9 constant_dynamic-slice_fusion
  9.5 0.0 all-gather.5.cloned.1.call-update
  9.5 0.0 copy-start.3
  9.5 0.0 all-gather.3.cloned.1.call-start
  9.6 0.7 all-gather.3.cloned.1.call-update
  10.9 0.0 copy-done.2
  10.9 0.0 copy-start.1
  11.0 1.9 %copy-done.1 = bf16[3,224,2432]{2,1,0:T(8,128)(2,1)S(1)} copy-done((bf16[3,224,2432]{2,1,0:T(8,128)(2,1)S(1)}, bf16[3,224,2432]{2,1,0:T(8,128)(2,1)}, u32[]{:S(2)}) %copy-start.1) | copy-done | bytes 3268632
  12.9 114.9 %attend.1 = (bf16[224,2432]{1,0:T(8,128)(2,1)S(1)}, bf16[64,2432]{1,0:T(8,128)(2,1)S(1)}) custom-call(bf16[3,224,2432]{2,1,0:T(8,128)(2,1)S(1)} %copy-done.1, bf16[3,16,2432]{2,1,0:T(8,128)(2,1)S(1)} %copy-done.2, f32[1,960]{1,0:T(1,128)S(1)} %or_select_fusion.bias), custom_call_target="tpu_custom_call" | custom-call | tf_op jit(solution)/shard_map/attend/pallas_call | solution.py:175
  127.7 0.0 copy-done.3
  127.8 0.1 dynamic-slice_reduce_fusion
  127.9 0.0 all-gather.5.cloned.1.call-done
  127.9 2.5 %fusion.1 = bf16[64,608]{1,0:T(8,128)(2,1)S(1)} fusion(bf16[64,2432]{1,0:T(8,128)(2,1)S(1)} %get-tuple-element.5, bf16[2432,608]{1,0:T(8,128)(2,1)} %all-gather.5.cloned.1.call-done, f32[608]{0:T(1024)S(1)} %dynamic-slice_reduce_fusion), kind=kOutput, calls=%fused_computation.3 | convolution fusion | flops 189345792 | bytes 3348864 | tf_op jit(solution)/shard_map/dot_general | solution.py:212
  130.5 8.2 %all_to_all.19 = bf16[4,16,608]{2,1,0:T(8,128)(2,1)S(1)} all-to-all(bf16[4,16,608]{2,1,0:T(8,128)(2,1)S(1)} %bitcast.8), channel_id=1, replica_groups=mesh['grp'=8,'blk'=4] {'blk'}, dimensions={0} | all-to-all | bytes 155648 | tf_op jit(solution)/shard_map/all_to_all | solution.py:214
  138.7 0.8 all_to_all.17
  139.4 0.0 all-gather.3.cloned.1.call-done
  139.4 8.5 %fusion = bf16[224,2432]{1,0:T(8,128)(2,1)} fusion(bf16[224,2432]{1,0:T(8,128)(2,1)S(1)} %get-tuple-element.4, bf16[2432,2432]{1,0:T(8,128)(2,1)} %all-gather.3.cloned.1.call-done, f32[2432]{0:T(1024)S(1)} %get-tuple-element.7), kind=kOutput, calls=%fused_computation.1 | convolution fusion | flops 2650841088 | bytes 14018048 | tf_op jit(solution)/shard_map/dot_general | solution.py:216
  (3 shorter events, 0.1 us)
Async XLA Ops:
  7.2 1.4 copy-start
  7.2 3.8 %copy-start.2 = (bf16[3,16,2432]{2,1,0:T(8,128)(2,1)S(1)}, bf16[3,16,2432]{2,1,0:T(8,128)(2,1)}, u32[]{:S(2)}) copy-start(bf16[3,16,2432]{2,1,0:T(8,128)(2,1)} %txt.1) | copy-start | bytes 700420
  7.2 120.7 %all-gather.5.cloned.1.call-start = ((), (), s32[]{:S(2)}) async-start(), calls=%async_computation.2 | async-start | bytes 3502080 | tf_op jit(solution)/shard_map/all_gather | solution.py:208
  9.5 118.3 %copy-start.3 = (f32[1,2,2432]{2,1,0:T(2,128)S(1)}, f32[1,2,2432]{2,1,0:T(2,128)}, u32[]{:S(2)}) copy-start(f32[1,2,2432]{2,1,0:T(2,128)} %param.11) | copy-start | bytes 58372
  9.5 129.9 %all-gather.3.cloned.1.call-start = ((), (), s32[]{:S(2)}) async-start(), calls=%async_computation.1 | async-start | bytes 13307904 | tf_op jit(solution)/shard_map/all_gather | solution.py:207
  10.9 1.9 %copy-start.1 = (bf16[3,224,2432]{2,1,0:T(8,128)(2,1)S(1)}, bf16[3,224,2432]{2,1,0:T(8,128)(2,1)}, u32[]{:S(2)}) copy-start(bf16[3,224,2432]{2,1,0:T(8,128)(2,1)} %img.1) | copy-start | bytes 9805828
Sparse Core Ops, SparseCore 0:
  10.5 34.8 all-gather.4
  47.2 68.7 all-gather.2
